TPU v7x, 256 devices: a whole 4x4x8 slice. The times are simulated.
256 devices in a mesh: hid: 32 (over x, z), tok: 8 (over y, core).
Axes of the slice: x: 4, y: 4, z: 8, core: 2. Of those that a mesh axis runs over, the one named last changes fastest.
Arguments:
- tokens: bfloat16 [2048, 12288], P('tok', 'hid'), may hold values from -6 to 6
- cotangent: bfloat16 [2048, 12288], P('tok', 'hid'), may hold values from -0.75 to 0.75
- up_tiles: bfloat16 [6, 256, 24576], P(None, None, 'hid'), may hold values from -0.15625 to 0.15625
- down_tiles: bfloat16 [6, 24576, 256], P(None, 'hid'), may hold values from -0.109375 to 0.109375
- block_index: int32 [6, 96, 2], P(None, 'hid'), may hold values from 0 to 2, as said below
- up_left: bfloat16 [12288, 256], P('hid'), may hold values from -0.0546875 to 0.0546875
- up_right: bfloat16 [256, 24576], P(None, 'hid'), may hold values from -0.375 to 0.375
- down_left: bfloat16 [24576, 256], P('hid'), may hold values from -0.0390625 to 0.0390625
- down_right: bfloat16 [256, 12288], P(None, 'hid'), may hold values from -0.375 to 0.375
Outputs:
- layer_out: bfloat16 [2048, 12288], P('tok', 'hid')
- grad_tokens: bfloat16 [2048, 12288], P('tok', 'hid')
- grad_up_tiles: bfloat16 [6, 256, 24576], P(None, 'tok', 'hid')
- grad_down_tiles: bfloat16 [6, 24576, 256], P(None, ('hid', 'tok'))
- grad_up_left: bfloat16 [12288, 256], P(('hid', 'tok'))
- grad_up_right: bfloat16 [256, 24576], P('tok', 'hid')
- grad_down_left: bfloat16 [24576, 256], P(('hid', 'tok'))
- grad_down_right: bfloat16 [256, 12288], P('tok', 'hid')
Inputs may be any that keep to these rules, and one draw needn't show every extreme that they name: `block_index`: each row names two different sub-blocks.
All inputs are finite; a program needn't handle non-finite values.
Results may differ from a plain program's by a relative error of at most 0.03.
Values may be sent and summed in bfloat16 or wider, within the bound.
No kernel may reach another device: no remote copies, remote signals or barrier semaphores. Data moves between devices by JAX's collectives and lax.ppermute only.
A program may use at most 128 MiB of HBM per device.

v0:
```python
import jax
import jax.numpy as jnp
from jax import lax
from jax.sharding import PartitionSpec as P

GELU_SCALE = 0.7978845608028654
GELU_CUBIC = 0.044715


def partner(block, axis, distance):
    count = lax.axis_size(axis)
    route = []
    for low in range(count):
        high = low | 1 << distance
        if high != low and high < count:
            route += [(low, high), (high, low)]
    return lax.ppermute(block, axis, route)


def gelu_parts(pre_act):
    inner = GELU_SCALE * (pre_act + GELU_CUBIC * pre_act * pre_act * pre_act)
    tanh_value = jnp.tanh(inner)
    value = 0.5 * pre_act * (1.0 + tanh_value)
    slope = 0.5 * (1.0 + tanh_value) + 0.5 * pre_act * (
        1.0 - tanh_value * tanh_value
    ) * GELU_SCALE * (1.0 + 3.0 * GELU_CUBIC * pre_act * pre_act)
    return (value, slope)


def on_device(
    tokens, cotangent, up_tiles, down_tiles, block_index, up_left, up_right, down_left, down_right
):
    hid_count = lax.axis_size("hid")
    level_count = hid_count.bit_length()
    position = lax.axis_index("hid")
    token_rows, feat_width = tokens.shape
    sub_width = feat_width // 3
    block_count = block_index.shape[1]
    hidden_width = up_tiles.shape[2]
    block_width = hidden_width // block_count
    select_float_values = (block_index[..., None] == jnp.arange(3, dtype=jnp.int32)).astype(
        jnp.float32
    )
    select_half_values = select_float_values.astype(jnp.bfloat16)
    up_blocks = [
        up_tiles[partition_key].reshape(2, sub_width, block_count, block_width)
        for partition_key in range(level_count)
    ]
    down_blocks = [
        down_tiles[partition_key].reshape(block_count, block_width, 2, sub_width)
        for partition_key in range(level_count)
    ]

    def partner_of(partition_key):
        if partition_key == 0:
            return position
        return jnp.bitwise_xor(position, jnp.int32(1 << partition_key - 1))

    def choose(field, partition_key):
        reshaped_tiles = field.reshape(token_rows, 3, sub_width)
        return jnp.einsum(
            "rfg,hyf->rhyg",
            reshaped_tiles,
            select_half_values[partition_key],
            preferred_element_type=jnp.float32,
        ).astype(jnp.bfloat16)

    def place(partner_pairs, partition_key):
        placed_blocks = jnp.einsum(
            "kdow,dog->kgw",
            partner_pairs,
            select_float_values[partition_key],
            precision=lax.Precision.HIGHEST,
        )
        return placed_blocks.reshape(token_rows, feat_width).astype(jnp.bfloat16)

    gathered = lax.all_gather(tokens, "hid", axis=1, tiled=True)
    feature_copies = [
        lax.dynamic_slice_in_dim(gathered, partner_of(partition_key) * feat_width, feat_width, 1)
        for partition_key in range(level_count)
    ]
    low_up = lax.psum(
        jnp.dot(tokens, up_left, preferred_element_type=jnp.float32).astype(jnp.bfloat16), "hid"
    )
    chosen_inputs = [
        choose(feature_copies[partition_key], partition_key) for partition_key in range(level_count)
    ]
    pre_act = jnp.dot(low_up, up_right, preferred_element_type=jnp.float32).reshape(
        token_rows, block_count, block_width
    )
    for partition_key in range(level_count):
        pre_act = pre_act + jnp.einsum(
            "tbjs,jsbh->tbh",
            chosen_inputs[partition_key],
            up_blocks[partition_key],
            preferred_element_type=jnp.float32,
        )
    hidden_value, slope = gelu_parts(pre_act)
    hidden_act = hidden_value.astype(jnp.bfloat16)
    hidden_flat = hidden_act.reshape(token_rows, hidden_width)
    low_down = lax.psum(
        jnp.dot(hidden_flat, down_left, preferred_element_type=jnp.float32).astype(jnp.bfloat16),
        "hid",
    )
    out_parts = [
        place(
            jnp.einsum(
                "tbh,bhjs->tbjs",
                hidden_act,
                down_blocks[partition_key],
                preferred_element_type=jnp.float32,
            ),
            partition_key,
        )
        for partition_key in range(level_count)
    ]
    output_acc = out_parts[0].astype(jnp.float32)
    for partition_key in range(1, level_count):
        output_acc = output_acc + partner(
            out_parts[partition_key], "hid", partition_key - 1
        ).astype(jnp.float32)
    layer_out = (
        output_acc + jnp.dot(low_down, down_right, preferred_element_type=jnp.float32)
    ).astype(jnp.bfloat16)
    back_down = lax.psum(
        jnp.dot(cotangent, down_right.T, preferred_element_type=jnp.float32).astype(jnp.bfloat16),
        "hid",
    )
    grad_gathered = lax.all_gather(cotangent, "hid", axis=1, tiled=True)
    grad_copies = [
        lax.dynamic_slice_in_dim(
            grad_gathered, partner_of(partition_key) * feat_width, feat_width, 1
        )
        for partition_key in range(level_count)
    ]
    chosen_grads = [
        choose(grad_copies[partition_key], partition_key) for partition_key in range(level_count)
    ]
    grad_hidden = jnp.dot(back_down, down_left.T, preferred_element_type=jnp.float32).reshape(
        token_rows, block_count, block_width
    )
    for partition_key in range(level_count):
        grad_hidden = grad_hidden + jnp.einsum(
            "tbjs,bhjs->tbh",
            chosen_grads[partition_key],
            down_blocks[partition_key],
            preferred_element_type=jnp.float32,
        )
    down_terms = jnp.stack(
        [
            jnp.einsum(
                "tbh,tbjs->bhjs",
                hidden_act,
                chosen_grads[partition_key],
                preferred_element_type=jnp.float32,
            ).reshape(hidden_width, 2 * sub_width)
            for partition_key in range(level_count)
        ]
    )
    down_left_term = jnp.dot(hidden_flat.T, back_down, preferred_element_type=jnp.float32)
    down_right_term = jnp.dot(low_down.T, cotangent, preferred_element_type=jnp.float32)
    grad_down_tiles, grad_down_left, grad_down_right = (
        lax.psum_scatter(
            down_terms.astype(jnp.bfloat16), "tok", scatter_dimension=1, tiled=True
        ).astype(jnp.float32),
        lax.psum_scatter(
            down_left_term.astype(jnp.bfloat16), "tok", scatter_dimension=0, tiled=True
        ).astype(jnp.float32),
        lax.psum_scatter(
            down_right_term.astype(jnp.bfloat16), "tok", scatter_dimension=0, tiled=True
        ).astype(jnp.float32),
    )
    grad_pre = (grad_hidden * slope).astype(jnp.bfloat16)
    grad_flat = grad_pre.reshape(token_rows, hidden_width)
    back_up = lax.psum(
        jnp.dot(grad_flat, up_right.T, preferred_element_type=jnp.float32).astype(jnp.bfloat16),
        "hid",
    )
    in_parts = [
        place(
            jnp.einsum(
                "tbh,jsbh->tbjs",
                grad_pre,
                up_blocks[partition_key],
                preferred_element_type=jnp.float32,
            ),
            partition_key,
        )
        for partition_key in range(level_count)
    ]
    input_acc = in_parts[0].astype(jnp.float32)
    for partition_key in range(1, level_count):
        input_acc = input_acc + partner(in_parts[partition_key], "hid", partition_key - 1).astype(
            jnp.float32
        )
    grad_tokens = (
        input_acc + jnp.dot(back_up, up_left.T, preferred_element_type=jnp.float32)
    ).astype(jnp.bfloat16)
    up_terms = jnp.stack(
        [
            jnp.einsum(
                "tbjs,tbh->jsbh",
                chosen_inputs[partition_key],
                grad_pre,
                preferred_element_type=jnp.float32,
            ).reshape(2 * sub_width, hidden_width)
            for partition_key in range(level_count)
        ]
    )
    up_right_term = jnp.dot(low_up.T, grad_flat, preferred_element_type=jnp.float32)
    up_left_term = jnp.dot(tokens.T, back_up, preferred_element_type=jnp.float32)
    grad_up_tiles, grad_up_right, grad_up_left = (
        lax.psum_scatter(
            up_terms.astype(jnp.bfloat16), "tok", scatter_dimension=1, tiled=True
        ).astype(jnp.float32),
        lax.psum_scatter(
            up_right_term.astype(jnp.bfloat16), "tok", scatter_dimension=0, tiled=True
        ).astype(jnp.float32),
        lax.psum_scatter(
            up_left_term.astype(jnp.bfloat16), "tok", scatter_dimension=0, tiled=True
        ).astype(jnp.float32),
    )
    return (
        layer_out,
        grad_tokens,
        grad_up_tiles.astype(jnp.bfloat16),
        grad_down_tiles.astype(jnp.bfloat16),
        grad_up_left.astype(jnp.bfloat16),
        grad_up_right.astype(jnp.bfloat16),
        grad_down_left.astype(jnp.bfloat16),
        grad_down_right.astype(jnp.bfloat16),
    )


def solution(mesh):
    return jax.shard_map(
        on_device,
        mesh=mesh,
        in_specs=(
            P("tok", "hid"),
            P("tok", "hid"),
            P(None, None, "hid"),
            P(None, "hid", None),
            P(None, "hid", None),
            P("hid", None),
            P(None, "hid"),
            P("hid", None),
            P(None, "hid"),
        ),
        out_specs=(
            P("tok", "hid"),
            P("tok", "hid"),
            P(None, "tok", "hid"),
            P(None, ("hid", "tok"), None),
            P(("hid", "tok"), None),
            P("tok", "hid"),
            P(("hid", "tok"), None),
            P("tok", "hid"),
        ),
        check_vma=False,
    )
```

profile of v0, /device:TPU:2, one launch (start us, length us, event | category | flops | bytes accessed | tf_op | source)
XLA Modules:
  0.0 776.2 jit_solution(9446525643140161980)
XLA Ops:
  7.3 2.1 convolution_convert_fusion.29
  16.3 2.2 reshape.191
  18.5 2.1 reshape.190
  20.6 2.3 reshape.189
  25.1 2.5 fusion.172
  30.7 127.4 %all-reduce.7.cloned.1.call-done = (bf16[256,256]{1,0:T(8,128)(2,1)}, bf16[256,256]{1,0:T(8,128)(2,1)}) async-done(((bf16[256,256]{1,0:T(8,128)(2,1)}, bf16[256,256]{1,0:T(8,128)(2,1)}), (bf16[256,256]{1,0:T(8,128)(2,1)}, bf16[256,256]{1,0:T(8,128)(2,1)})) %all-reduce.7.cloned.1.call-update) | async-done | bytes 262160 | tf_op jit(solution)/shard_map/psum | solution.py:82
  158.1 2.1 fusion.175
  160.2 2.2 fusion.176
  162.5 84.4 %all-gather.3.cloned.1.call-done = bf16[256,12288]{0,1:T(8,128)(2,1)} async-done(((bf16[256,384]{0,1:T(8,128)(2,1)}), bf16[256,12288]{0,1:T(8,128)(2,1)}) %all-gather.3.cloned.1.call-update) | async-done | bytes 6291472 | tf_op jit(solution)/shard_map/all_gather | solution.py:77
  246.9 88.8 %all-gather.5.cloned.1.call-done = bf16[256,12288]{0,1:T(8,128)(2,1)} async-done(((bf16[256,384]{0,1:T(8,128)(2,1)}), bf16[256,12288]{0,1:T(8,128)(2,1)}) %all-gather.5.cloned.1.call-update) | async-done | bytes 6291472 | tf_op jit(solution)/shard_map/all_gather | solution.py:129
  335.7 3.0 constant_dynamic-slice_fusion.5
  363.7 2.1 fusion.22
  369.7 2.1 fusion.23
  375.6 2.1 fusion.24
  400.2 2.1 copy.346
  413.9 4.9 copy.351
  423.4 2.1 fusion.52
  426.2 124.4 %all-reduce.5.cloned.1.call-done = (bf16[256,256]{1,0:T(8,128)(2,1)}, bf16[256,256]{1,0:T(8,128)(2,1)}) async-done(((bf16[256,256]{1,0:T(8,128)(2,1)}, bf16[256,256]{1,0:T(8,128)(2,1)}), (bf16[256,256]{1,0:T(8,128)(2,1)}, bf16[256,256]{1,0:T(8,128)(2,1)})) %all-reduce.5.cloned.1.call-update) | async-done | bytes 262160 | tf_op jit(solution)/shard_map/psum | solution.py:101
  554.2 2.1 convolution_convert_fusion.15
  560.2 2.2 fusion.36
  562.7 2.1 convolution_convert_fusion.14
  569.3 2.2 copy.359
  573.6 2.2 copy.361
  577.8 2.2 copy.363
  595.5 2.1 fusion.50
  599.6 2.5 collective-permute-start.7
  633.9 3.1 collective-permute-start.2
  641.7 4.1 collective-permute-done.1
  649.2 10.5 %reduce-scatter.17.cloned.1.call-done = bf16[32,384]{1,0:T(8,128)(2,1)} async-done(((bf16[256,384]{1,0:T(8,128)(2,1)}), bf16[32,384]{1,0:T(8,128)(2,1)}) %reduce-scatter.17.cloned.1.call-update) | async-done | bytes 24592 | tf_op jit(solution)/shard_map/reduce_scatter | solution.py:169
  659.8 35.3 %reduce-scatter.13.cloned.1.call-done = bf16[32,768]{1,0:T(8,128)(2,1)} async-done(((bf16[256,768]{1,0:T(8,128)(2,1)}), bf16[32,768]{1,0:T(8,128)(2,1)}) %reduce-scatter.13.cloned.1.call-update) | async-done | bytes 49168 | tf_op jit(solution)/shard_map/reduce_scatter | solution.py:216
  695.0 35.5 %reduce-scatter.15.cloned.1.call-done = bf16[96,256]{1,0:T(8,128)(2,1)} async-done(((bf16[768,256]{1,0:T(8,128)(2,1)}), bf16[96,256]{1,0:T(8,128)(2,1)}) %reduce-scatter.15.cloned.1.call-update) | async-done | bytes 49168 | tf_op jit(solution)/shard_map/reduce_scatter | solution.py:166
  730.5 38.6 %reduce-scatter.11.cloned.1.call-done = bf16[6,96,256]{2,1,0:T(8,128)(2,1)} async-done(((bf16[6,768,256]{2,1,0:T(8,128)(2,1)}), bf16[6,96,256]{2,1,0:T(8,128)(2,1)}) %reduce-scatter.11.cloned.1.call-update) | async-done | bytes 294928 | tf_op jit(solution)/shard_map/reduce_scatter | solution.py:163
  (305 shorter events, 156.9 us)
Async XLA Ops:
  7.2 150.9 %copy-start = (bf16[256,768]{1,0:T(8,128)(2,1)S(1)}, bf16[256,768]{1,0:T(8,128)(2,1)}, u32[]{:S(2)}) copy-start(bf16[256,768]{1,0:T(8,128)(2,1)} %param.15) | copy-start | bytes 1179652
  7.2 150.9 %all-reduce.7.cloned.1.call-start = ((), (), s32[]{:S(2)}) async-start(), calls=%async_computation.15 | async-start | bytes 524288 | tf_op jit(solution)/shard_map/psum | solution.py:82
  11.3 235.6 %all-gather.3.cloned.1.call-start = ((), (), s32[]{:S(2)}) async-start(), calls=%async_computation.6 | async-start | bytes 6488064 | tf_op jit(solution)/shard_map/all_gather | solution.py:77
  13.1 322.6 %all-gather.5.cloned.1.call-start = ((), (), s32[]{:S(2)}) async-start(), calls=%async_computation.7 | async-start | bytes 6488064 | tf_op jit(solution)/shard_map/all_gather | solution.py:129
  14.9 535.6 %all-reduce.5.cloned.1.call-start = ((), (), s32[]{:S(2)}) async-start(), calls=%async_computation.14 | async-start | bytes 524288 | tf_op jit(solution)/shard_map/psum | solution.py:101
  23.1 360.5 %copy-start.10 = (bf16[2,128,3,256]{3,2,1,0:T(4,128)(2,1)}, bf16[2,128,3,256]{3,2,1,0:T(4,128)(2,1)S(1)}, u32[]{:S(2)}) copy-start(bf16[2,128,3,256]{3,2,1,0:T(4,128)(2,1)S(1)} %reshape.192) | copy-start | bytes 1179652
  27.9 356.9 %copy-start.2 = (bf16[3,256,2,128]{3,2,1,0:T(2,128)(2,1)}, bf16[3,256,2,128]{3,2,1,0:T(2,128)(2,1)S(1)}, u32[]{:S(2)}) copy-start(bf16[3,256,2,128]{3,2,1,0:T(2,128)(2,1)S(1)} %reshape_squeeze.46) | copy-start | bytes 1179652
  28.0 357.1 %copy-start.4 = (bf16[3,256,2,128]{3,2,1,0:T(2,128)(2,1)}, bf16[3,256,2,128]{3,2,1,0:T(2,128)(2,1)S(1)}, u32[]{:S(2)}) copy-start(bf16[3,256,2,128]{3,2,1,0:T(2,128)(2,1)S(1)} %reshape_squeeze.45) | copy-start | bytes 1179652
  28.1 357.4 %copy-start.6 = (bf16[3,256,2,128]{3,2,1,0:T(2,128)(2,1)}, bf16[3,256,2,128]{3,2,1,0:T(2,128)(2,1)S(1)}, u32[]{:S(2)}) copy-start(bf16[3,256,2,128]{3,2,1,0:T(2,128)(2,1)S(1)} %reshape_squeeze.44) | copy-start | bytes 1179652
  28.2 357.7 %copy-start.8 = (bf16[3,256,2,128]{3,2,1,0:T(2,128)(2,1)}, bf16[3,256,2,128]{3,2,1,0:T(2,128)(2,1)S(1)}, u32[]{:S(2)}) copy-start(bf16[3,256,2,128]{3,2,1,0:T(2,128)(2,1)S(1)} %reshape_squeeze.43) | copy-start | bytes 1179652
  359.8 13.8 %copy-start.56 = (bf16[3,2,3,1]{2,1,0,3:T(2,128)(2,1)S(1)}, bf16[3,2,3,1]{2,1,0,3:T(2,128)(2,1)}, u32[]{:S(2)}) copy-start(bf16[3,2,3,1]{2,1,0,3:T(2,128)(2,1)} %get-tuple-element.77) | copy-start | bytes 112
  409.2 238.3 %reduce-scatter.9.cloned.1.call-start = ((), (), s32[]{:S(2)}) async-start(), calls=%async_computation.8 | async-start | bytes 3538944 | tf_op jit(solution)/shard_map/reduce_scatter | solution.py:213
  418.8 230.4 %reduce-scatter.19.cloned.1.call-start = ((), (), s32[]{:S(2)}) async-start(), calls=%async_computation.13 | async-start | bytes 221184
  423.4 127.2 %copy-start.39 = (bf16[256,384]{1,0:T(8,128)(2,1)S(1)}, bf16[256,384]{1,0:T(8,128)(2,1)}, u32[]{:S(2)}) copy-start(bf16[256,384]{1,0:T(8,128)(2,1)} %param.9) | copy-start | bytes 589828
  425.5 130.8 %copy-start.40 = (bf16[256,384]{1,0:T(8,128)(2,1)S(1)}, bf16[256,384]{1,0:T(8,128)(2,1)}, u32[]{:S(2)}) copy-start(bf16[256,384]{1,0:T(8,128)(2,1)} %param.10) | copy-start | bytes 589828
  554.1 105.6 %reduce-scatter.17.cloned.1.call-start = ((), (), s32[]{:S(2)}) async-start(), calls=%async_computation.12 | async-start | bytes 221184 | tf_op jit(solution)/shard_map/reduce_scatter | solution.py:169
  558.2 136.9 %reduce-scatter.13.cloned.1.call-start = ((), (), s32[]{:S(2)}) async-start(), calls=%async_computation.10 | async-start | bytes 442368 | tf_op jit(solution)/shard_map/reduce_scatter | solution.py:216
  562.5 168.0 %reduce-scatter.15.cloned.1.call-start = ((), (), s32[]{:S(2)}) async-start(), calls=%async_computation.11 | async-start | bytes 442368 | tf_op jit(solution)/shard_map/reduce_scatter | solution.py:166
  587.6 44.5 %collective-permute-start.5 = (bf16[256,384]{1,0:T(8,128)(2,1)}, bf16[256,384]{1,0:T(8,128)(2,1)}, u32[]{:S(2)}, u32[]{:S(2)}) collective-permute-start(bf16[256,384]{1,0:T(8,128)(2,1)} %copy.313), channel_id=1, source_target_pairs={{0,8},{8,0},{16,24},{24,16},{32,40},{40,32},{48,56},{56,48},{64,72... | collective-permute-start | bytes 589832 | tf_op jit(solution)/shard_map/ppermute | solution.py:17
  591.1 41.5 %collective-permute-start.6 = (bf16[256,384]{1,0:T(8,128)(2,1)}, bf16[256,384]{1,0:T(8,128)(2,1)}, u32[]{:S(2)}, u32[]{:S(2)}) collective-permute-start(bf16[256,384]{1,0:T(8,128)(2,1)} %copy.320), channel_id=1, source_target_pairs={{0,16},{16,0},{8,24},{24,8},{32,48},{48,32},{40,56},{56,40},{64,80... | collective-permute-start | bytes 589832 | tf_op jit(solution)/shard_map/ppermute | solution.py:17
  595.4 173.7 %reduce-scatter.11.cloned.1.call-start = ((), (), s32[]{:S(2)}) async-start(), calls=%async_computation.9 | async-start | bytes 2654208 | tf_op jit(solution)/shard_map/reduce_scatter | solution.py:163
  599.6 34.3 %collective-permute-start.7 = (bf16[256,384]{1,0:T(8,128)(2,1)}, bf16[256,384]{1,0:T(8,128)(2,1)}, u32[]{:S(2)}, u32[]{:S(2)}) collective-permute-start(bf16[256,384]{1,0:T(8,128)(2,1)} %copy.326), channel_id=1, source_target_pairs={{0,32},{32,0},{8,40},{40,8},{16,48},{48,16},{24,56},{56,24},{64,96... | collective-permute-start | bytes 589832 | tf_op jit(solution)/shard_map/ppermute | solution.py:17
  610.0 26.9 %collective-permute-start.8 = (bf16[256,384]{1,0:T(8,128)(2,1)S(1)}, bf16[256,384]{1,0:T(8,128)(2,1)S(1)}, u32[]{:S(2)}, u32[]{:S(2)}) collective-permute-start(bf16[256,384]{1,0:T(8,128)(2,1)S(1)} %copy.332), channel_id=1, source_target_pairs={{0,64},{64,0},{8,72},{72,8},{16,80},{80,16},{24,88},{88,24},{32,96... | collective-permute-start | bytes 589832 | tf_op jit(solution)/shard_map/ppermute | solution.py:17
  614.6 24.2 %collective-permute-start.9 = (bf16[256,384]{1,0:T(8,128)(2,1)}, bf16[256,384]{1,0:T(8,128)(2,1)S(1)}, u32[]{:S(2)}, u32[]{:S(2)}) collective-permute-start(bf16[256,384]{1,0:T(8,128)(2,1)} %copy.338), channel_id=1, source_target_pairs={{0,128},{128,0},{8,136},{136,8},{16,144},{144,16},{24,152},{152,24... | collective-permute-start | bytes 589832 | tf_op jit(solution)/shard_map/ppermute | solution.py:17
  629.5 17.0 %copy-start.52 = (bf16[256,384]{1,0:T(8,128)(2,1)S(1)}, bf16[256,384]{1,0:T(8,128)(2,1)}, u32[]{:S(2)}) copy-start(bf16[256,384]{1,0:T(8,128)(2,1)} %param.17) | copy-start | bytes 589828
  629.6 17.0 %copy-start.53 = (bf16[256,256]{1,0:T(8,128)(2,1)S(1)}, bf16[256,256]{1,0:T(8,128)(2,1)}, u32[]{:S(2)}) copy-start(bf16[256,256]{1,0:T(8,128)(2,1)} %get-tuple-element.32) | copy-start | bytes 393220
  631.2 137.9 %copy-start.1 = (bf16[256,768]{1,0:T(8,128)(2,1)S(1)}, bf16[256,768]{1,0:T(8,128)(2,1)}, u32[]{:S(2)}) copy-start(bf16[256,768]{1,0:T(8,128)(2,1)} %param.15) | copy-start | bytes 1179652
  632.0 9.7 %collective-permute-start = (bf16[256,384]{1,0:T(8,128)(2,1)}, bf16[256,384]{1,0:T(8,128)(2,1)S(1)}, u32[]{:S(2)}, u32[]{:S(2)}) collective-permute-start(bf16[256,384]{1,0:T(8,128)(2,1)} %copy.251), channel_id=1, source_target_pairs={{0,8},{8,0},{16,24},{24,16},{32,40},{40,32},{48,56},{56,48},{64,72... | collective-permute-start | bytes 589832 | tf_op jit(solution)/shard_map/ppermute | solution.py:17
  632.6 13.2 %collective-permute-start.1 = (bf16[256,384]{1,0:T(8,128)(2,1)}, bf16[256,384]{1,0:T(8,128)(2,1)S(1)}, u32[]{:S(2)}, u32[]{:S(2)}) collective-permute-start(bf16[256,384]{1,0:T(8,128)(2,1)} %copy.258), channel_id=1, source_target_pairs={{0,16},{16,0},{8,24},{24,8},{32,48},{48,32},{40,56},{56,40},{64,80... | collective-permute-start | bytes 589832 | tf_op jit(solution)/shard_map/ppermute | solution.py:17
  633.9 12.6 %collective-permute-start.2 = (bf16[256,384]{1,0:T(8,128)(2,1)}, bf16[256,384]{1,0:T(8,128)(2,1)S(1)}, u32[]{:S(2)}, u32[]{:S(2)}) collective-permute-start(bf16[256,384]{1,0:T(8,128)(2,1)} %copy.264), channel_id=1, source_target_pairs={{0,32},{32,0},{8,40},{40,8},{16,48},{48,16},{24,56},{56,24},{64,96... | collective-permute-start | bytes 589832 | tf_op jit(solution)/shard_map/ppermute | solution.py:17
  637.0 9.6 %collective-permute-start.3 = (bf16[256,384]{1,0:T(8,128)(2,1)}, bf16[256,384]{1,0:T(8,128)(2,1)S(1)}, u32[]{:S(2)}, u32[]{:S(2)}) collective-permute-start(bf16[256,384]{1,0:T(8,128)(2,1)} %copy.270), channel_id=1, source_target_pairs={{0,64},{64,0},{8,72},{72,8},{16,80},{80,16},{24,88},{88,24},{32,96... | collective-permute-start | bytes 589832 | tf_op jit(solution)/shard_map/ppermute | solution.py:17
  638.7 7.8 %collective-permute-start.4 = (bf16[256,384]{1,0:T(8,128)(2,1)}, bf16[256,384]{1,0:T(8,128)(2,1)S(1)}, u32[]{:S(2)}, u32[]{:S(2)}) collective-permute-start(bf16[256,384]{1,0:T(8,128)(2,1)} %copy.276), channel_id=1, source_target_pairs={{0,128},{128,0},{8,136},{136,8},{16,144},{144,16},{24,152},{152,24... | collective-permute-start | bytes 589832 | tf_op jit(solution)/shard_map/ppermute | solution.py:17
  (46 other events, 223.9 us)
Sparse Core Ops, SparseCore 0:
  12.1 145.9 all-reduce.6
  161.3 85.5 all-gather.2
  250.0 85.6 all-gather.4
  409.3 141.2 all-reduce.4
  552.9 36.3 reduce-scatter.8
  592.3 32.1 reduce-scatter.18
  627.7 32.0 reduce-scatter.16
  662.8 32.1 reduce-scatter.12
  698.3 32.1 reduce-scatter.14
  733.5 35.5 reduce-scatter.10
where the time goes:
time: 781 us; the launch traced here: 776 us
  waiting for transfers between devices  550 us (70%)
  local copies, waits for them, and re-layouts  106 us (14%)
  matrix products  87.5 us (11%)
  starting transfers between devices  17 us (2%)
  between operations  15.4 us (2%)
    psum x1, waiting for transfers between devices, on_device(): lax.psum(jnp.dot(tokens, up_left, preferred_element_type=jnp.float32).ast...  127 us
    psum x1, waiting for transfers between devices, on_device(): lax.psum(jnp.dot(hidden_flat, down_left, preferred_element_type=jnp.float...  124 us
    all_gather x1, waiting for transfers between devices, on_device(): grad_gathered = lax.all_gather(cotangent, 'hid', axis=1, tiled=True)  88.8 us
    all_gather x1, waiting for transfers between devices, on_device(): gathered = lax.all_gather(tokens, 'hid', axis=1, tiled=True)  84.4 us
    reduce_scatter x1, waiting for transfers between devices, on_device(): lax.psum_scatter(down_terms.astype(jnp.bfloat16), 'tok', scatter_dimensio...  38.6 us
    reduce_scatter x1, waiting for transfers between devices, on_device(): lax.psum_scatter(down_left_term.astype(jnp.bfloat16), 'tok', scatter_dime...  35.5 us
    reduce_scatter x1, waiting for transfers between devices, on_device(): lax.psum_scatter(up_right_term.astype(jnp.bfloat16), 'tok', scatter_dimen...  35.3 us
    dot_general x12, matrix products, choose(): jnp.einsum('rfg,hyf->rhyg', reshaped_tiles, select_half_values[partition_...  22.3 us
  transfers between devices with their start and end apart: 20, of which 10 were waited for; matrix products, arithmetic and copies ran while one was open for 15% of the time, Pallas kernels for 0%

commit v1 on v0

--- a/solution.py
+++ b/solution.py
@@ -126,7 +126,9 @@
         jnp.dot(cotangent, down_right.T, preferred_element_type=jnp.float32).astype(jnp.bfloat16),
         "hid",
     )
-    grad_gathered = lax.all_gather(cotangent, "hid", axis=1, tiled=True)
+    grad_gathered = jnp.concatenate(
+        lax.all_to_all(jnp.stack([cotangent] * lax.axis_size("hid")), "hid", 0, 0), axis=1
+    )
     grad_copies = [
         lax.dynamic_slice_in_dim(
             grad_gathered, partner_of(partition_key) * feat_width, feat_width, 1

time: 781 us -> 731 us (0.936)
  waiting for transfers between devices: 550 us -> 487 us
  starting transfers between devices: 17 us -> 28.9 us
    all_gather x1 -> x0, waiting for transfers between devices: 88.8 us -> none  [on_device(): grad_gathered = lax.all_gather(cotangent, 'hid', axis=1, tiled=True)]
    psum x1, waiting for transfers between devices: 127 us -> 153 us  [on_device(): lax.psum(jnp.dot(tokens, up_left, preferred_element_type=jnp.float32).ast...]
    all_to_all x0 -> x1, starting transfers between devices: none -> 11.9 us  [on_device(): lax.all_to_all(jnp.stack([cotangent] * lax.axis_size('hid')), 'hid', 0, 0)]
    unnamed x131 -> x133, local copies, waits for them, and re-layouts: 17.7 us -> 16.1 us
  transfers between devices with their start and end apart: 20 -> 20, of which waited for: 10 -> 9; matrix products, arithmetic and copies ran while one was open for 15% -> 16% of each run, Pallas kernels for 0% -> 0%
where the time goes in v1:
time: 731 us; the launch traced here: 726 us
  waiting for transfers between devices  487 us (67%)
  local copies, waits for them, and re-layouts  108 us (15%)
  matrix products  87.4 us (12%)
  starting transfers between devices  28.9 us (4%)
  between operations  15 us (2%)
    psum x1, waiting for transfers between devices, on_device(): lax.psum(jnp.dot(tokens, up_left, preferred_element_type=jnp.float32).ast...  153 us
    psum x1, waiting for transfers between devices, on_device(): lax.psum(jnp.dot(hidden_flat, down_left, preferred_element_type=jnp.float...  124 us
    all_gather x1, waiting for transfers between devices, on_device(): gathered = lax.all_gather(tokens, 'hid', axis=1, tiled=True)  84.4 us
    reduce_scatter x1, waiting for transfers between devices, on_device(): lax.psum_scatter(down_terms.astype(jnp.bfloat16), 'tok', scatter_dimensio...  38.8 us
    reduce_scatter x1, waiting for transfers between devices, on_device(): lax.psum_scatter(down_left_term.astype(jnp.bfloat16), 'tok', scatter_dime...  35.4 us
    reduce_scatter x1, waiting for transfers between devices, on_device(): lax.psum_scatter(up_right_term.astype(jnp.bfloat16), 'tok', scatter_dimen...  35.3 us
    dot_general x12, matrix products, choose(): jnp.einsum('rfg,hyf->rhyg', reshaped_tiles, select_half_values[partition_...  22.3 us
    reshape x12, local copies, waits for them, and re-layouts, choose(): reshaped_tiles = field.reshape(token_rows, 3, sub_width)  19.9 us
  transfers between devices with their start and end apart: 20, of which 9 were waited for; matrix products, arithmetic and copies ran while one was open for 16% of the time, Pallas kernels for 0%

profile of v1, /device:TPU:2, one launch (start us, length us, event | category | flops | bytes accessed | tf_op | source)
XLA Modules:
  0.0 725.8 jit_solution(15182358376455224441)
XLA Ops:
  12.2 3.3 stack.8
  15.5 11.9 %all-to-all-start = ((bf16[32,256,384]{1,2,0:T(8,128)(2,1)}), bf16[32,256,384]{1,2,0:T(8,128)(2,1)}, u32[]{:S(2)}, u32[]{:S(2)}) async-start(bf16[32,256,384]{1,2,0:T(8,128)(2,1)} %stack.8), calls=%async_computation | async-start | bytes 12582912 | tf_op jit(solution)/shard_map/all_to_all | solution.py:130
  29.7 2.2 reshape.201
  31.9 2.1 reshape.200
  34.1 2.3 reshape.199
  38.6 2.5 fusion.172
  44.1 152.9 %all-reduce.7.cloned.1.call-done = (bf16[256,256]{1,0:T(8,128)(2,1)}, bf16[256,256]{1,0:T(8,128)(2,1)}) async-done(((bf16[256,256]{1,0:T(8,128)(2,1)}, bf16[256,256]{1,0:T(8,128)(2,1)}), (bf16[256,256]{1,0:T(8,128)(2,1)}, bf16[256,256]{1,0:T(8,128)(2,1)})) %all-reduce.7.cloned.1.call-update) | async-done | bytes 262160 | tf_op jit(solution)/shard_map/psum | solution.py:82
  197.0 2.1 fusion.175
  199.1 2.3 fusion.176
  201.4 84.4 %all-gather.2.cloned.1.call-done = bf16[256,12288]{0,1:T(8,128)(2,1)} async-done(((bf16[256,384]{0,1:T(8,128)(2,1)}), bf16[256,12288]{0,1:T(8,128)(2,1)}) %all-gather.2.cloned.1.call-update) | async-done | bytes 6291472 | tf_op jit(solution)/shard_map/all_gather | solution.py:77
  285.8 3.0 constant_dynamic-slice_fusion.5
  313.6 2.1 fusion.22
  319.6 2.1 fusion.23
  325.5 2.1 fusion.24
  350.1 2.1 copy.346
  363.8 4.9 copy.351
  373.2 2.1 fusion.52
  376.0 124.4 %all-reduce.5.cloned.1.call-done = (bf16[256,256]{1,0:T(8,128)(2,1)}, bf16[256,256]{1,0:T(8,128)(2,1)}) async-done(((bf16[256,256]{1,0:T(8,128)(2,1)}, bf16[256,256]{1,0:T(8,128)(2,1)}), (bf16[256,256]{1,0:T(8,128)(2,1)}, bf16[256,256]{1,0:T(8,128)(2,1)})) %all-reduce.5.cloned.1.call-update) | async-done | bytes 262160 | tf_op jit(solution)/shard_map/psum | solution.py:101
  504.1 2.1 convolution_convert_fusion.15
  510.1 2.2 fusion.36
  512.6 2.1 convolution_convert_fusion.14
  519.2 2.2 copy.359
  523.4 2.2 copy.361
  527.7 2.2 copy.363
  545.4 2.1 fusion.50
  549.5 2.5 collective-permute-start.7
  583.8 3.1 collective-permute-start.2
  591.6 4.1 collective-permute-done.1
  599.1 10.4 %reduce-scatter.17.cloned.1.call-done = bf16[32,384]{1,0:T(8,128)(2,1)} async-done(((bf16[256,384]{1,0:T(8,128)(2,1)}), bf16[32,384]{1,0:T(8,128)(2,1)}) %reduce-scatter.17.cloned.1.call-update) | async-done | bytes 24592 | tf_op jit(solution)/shard_map/reduce_scatter | solution.py:171
  609.5 35.3 %reduce-scatter.13.cloned.1.call-done = bf16[32,768]{1,0:T(8,128)(2,1)} async-done(((bf16[256,768]{1,0:T(8,128)(2,1)}), bf16[32,768]{1,0:T(8,128)(2,1)}) %reduce-scatter.13.cloned.1.call-update) | async-done | bytes 49168 | tf_op jit(solution)/shard_map/reduce_scatter | solution.py:218
  644.8 35.4 %reduce-scatter.15.cloned.1.call-done = bf16[96,256]{1,0:T(8,128)(2,1)} async-done(((bf16[768,256]{1,0:T(8,128)(2,1)}), bf16[96,256]{1,0:T(8,128)(2,1)}) %reduce-scatter.15.cloned.1.call-update) | async-done | bytes 49168 | tf_op jit(solution)/shard_map/reduce_scatter | solution.py:168
  680.2 38.8 %reduce-scatter.11.cloned.1.call-done = bf16[6,96,256]{2,1,0:T(8,128)(2,1)} async-done(((bf16[6,768,256]{2,1,0:T(8,128)(2,1)}), bf16[6,96,256]{2,1,0:T(8,128)(2,1)}) %reduce-scatter.11.cloned.1.call-update) | async-done | bytes 294928 | tf_op jit(solution)/shard_map/reduce_scatter | solution.py:165
  (307 shorter events, 157.0 us)
Async XLA Ops:
  7.2 189.8 %copy-start = (bf16[256,768]{1,0:T(8,128)(2,1)S(1)}, bf16[256,768]{1,0:T(8,128)(2,1)}, u32[]{:S(2)}) copy-start(bf16[256,768]{1,0:T(8,128)(2,1)} %param.15) | copy-start | bytes 1179652
  7.2 189.8 %all-reduce.7.cloned.1.call-start = ((), (), s32[]{:S(2)}) async-start(), calls=%async_computation.15 | async-start | bytes 524288 | tf_op jit(solution)/shard_map/psum | solution.py:82
  15.5 185.9 %all-to-all-start = ((bf16[32,256,384]{1,2,0:T(8,128)(2,1)}), bf16[32,256,384]{1,2,0:T(8,128)(2,1)}, u32[]{:S(2)}, u32[]{:S(2)}) async-start(bf16[32,256,384]{1,2,0:T(8,128)(2,1)} %stack.8), calls=%async_computation | async-start | bytes 12582912 | tf_op jit(solution)/shard_map/all_to_all | solution.py:130
  27.4 258.3 %all-gather.2.cloned.1.call-start = ((), (), s32[]{:S(2)}) async-start(), calls=%async_computation.7 | async-start | bytes 6488064 | tf_op jit(solution)/shard_map/all_gather | solution.py:77
  28.3 472.1 %all-reduce.5.cloned.1.call-start = ((), (), s32[]{:S(2)}) async-start(), calls=%async_computation.14 | async-start | bytes 524288 | tf_op jit(solution)/shard_map/psum | solution.py:101
  36.5 297.0 %copy-start.10 = (bf16[2,128,3,256]{3,2,1,0:T(4,128)(2,1)}, bf16[2,128,3,256]{3,2,1,0:T(4,128)(2,1)S(1)}, u32[]{:S(2)}) copy-start(bf16[2,128,3,256]{3,2,1,0:T(4,128)(2,1)S(1)} %reshape.202) | copy-start | bytes 1179652
  41.3 293.4 %copy-start.2 = (bf16[3,256,2,128]{3,2,1,0:T(2,128)(2,1)}, bf16[3,256,2,128]{3,2,1,0:T(2,128)(2,1)S(1)}, u32[]{:S(2)}) copy-start(bf16[3,256,2,128]{3,2,1,0:T(2,128)(2,1)S(1)} %reshape_squeeze.46) | copy-start | bytes 1179652
  41.4 293.6 %copy-start.4 = (bf16[3,256,2,128]{3,2,1,0:T(2,128)(2,1)}, bf16[3,256,2,128]{3,2,1,0:T(2,128)(2,1)S(1)}, u32[]{:S(2)}) copy-start(bf16[3,256,2,128]{3,2,1,0:T(2,128)(2,1)S(1)} %reshape_squeeze.45) | copy-start | bytes 1179652
  41.5 293.9 %copy-start.6 = (bf16[3,256,2,128]{3,2,1,0:T(2,128)(2,1)}, bf16[3,256,2,128]{3,2,1,0:T(2,128)(2,1)S(1)}, u32[]{:S(2)}) copy-start(bf16[3,256,2,128]{3,2,1,0:T(2,128)(2,1)S(1)} %reshape_squeeze.44) | copy-start | bytes 1179652
  41.6 294.2 %copy-start.8 = (bf16[3,256,2,128]{3,2,1,0:T(2,128)(2,1)}, bf16[3,256,2,128]{3,2,1,0:T(2,128)(2,1)S(1)}, u32[]{:S(2)}) copy-start(bf16[3,256,2,128]{3,2,1,0:T(2,128)(2,1)S(1)} %reshape_squeeze.43) | copy-start | bytes 1179652
  309.7 13.7 %copy-start.57 = (bf16[3,2,3,1]{2,1,0,3:T(2,128)(2,1)S(1)}, bf16[3,2,3,1]{2,1,0,3:T(2,128)(2,1)}, u32[]{:S(2)}) copy-start(bf16[3,2,3,1]{2,1,0,3:T(2,128)(2,1)} %get-tuple-element.77) | copy-start | bytes 112
  359.1 238.3 %reduce-scatter.9.cloned.1.call-start = ((), (), s32[]{:S(2)}) async-start(), calls=%async_computation.8 | async-start | bytes 3538944 | tf_op jit(solution)/shard_map/reduce_scatter | solution.py:215
  368.7 230.4 %reduce-scatter.19.cloned.1.call-start = ((), (), s32[]{:S(2)}) async-start(), calls=%async_computation.13 | async-start | bytes 221184
  373.2 127.2 %copy-start.40 = (bf16[256,384]{1,0:T(8,128)(2,1)S(1)}, bf16[256,384]{1,0:T(8,128)(2,1)}, u32[]{:S(2)}) copy-start(bf16[256,384]{1,0:T(8,128)(2,1)} %param.9) | copy-start | bytes 589828
  375.4 130.8 %copy-start.41 = (bf16[256,384]{1,0:T(8,128)(2,1)S(1)}, bf16[256,384]{1,0:T(8,128)(2,1)}, u32[]{:S(2)}) copy-start(bf16[256,384]{1,0:T(8,128)(2,1)} %param.10) | copy-start | bytes 589828
  504.0 105.5 %reduce-scatter.17.cloned.1.call-start = ((), (), s32[]{:S(2)}) async-start(), calls=%async_computation.12 | async-start | bytes 221184 | tf_op jit(solution)/shard_map/reduce_scatter | solution.py:171
  508.1 136.7 %reduce-scatter.13.cloned.1.call-start = ((), (), s32[]{:S(2)}) async-start(), calls=%async_computation.10 | async-start | bytes 442368 | tf_op jit(solution)/shard_map/reduce_scatter | solution.py:218
  512.4 167.8 %reduce-scatter.15.cloned.1.call-start = ((), (), s32[]{:S(2)}) async-start(), calls=%async_computation.11 | async-start | bytes 442368 | tf_op jit(solution)/shard_map/reduce_scatter | solution.py:168
  537.4 44.5 %collective-permute-start.5 = (bf16[256,384]{1,0:T(8,128)(2,1)}, bf16[256,384]{1,0:T(8,128)(2,1)}, u32[]{:S(2)}, u32[]{:S(2)}) collective-permute-start(bf16[256,384]{1,0:T(8,128)(2,1)} %copy.313), channel_id=1, source_target_pairs={{0,8},{8,0},{16,24},{24,16},{32,40},{40,32},{48,56},{56,48},{64,72... | collective-permute-start | bytes 589832 | tf_op jit(solution)/shard_map/ppermute | solution.py:17
  541.0 41.5 %collective-permute-start.6 = (bf16[256,384]{1,0:T(8,128)(2,1)}, bf16[256,384]{1,0:T(8,128)(2,1)}, u32[]{:S(2)}, u32[]{:S(2)}) collective-permute-start(bf16[256,384]{1,0:T(8,128)(2,1)} %copy.320), channel_id=1, source_target_pairs={{0,16},{16,0},{8,24},{24,8},{32,48},{48,32},{40,56},{56,40},{64,80... | collective-permute-start | bytes 589832 | tf_op jit(solution)/shard_map/ppermute | solution.py:17
  545.4 173.6 %reduce-scatter.11.cloned.1.call-start = ((), (), s32[]{:S(2)}) async-start(), calls=%async_computation.9 | async-start | bytes 2654208 | tf_op jit(solution)/shard_map/reduce_scatter | solution.py:165
  549.5 34.3 %collective-permute-start.7 = (bf16[256,384]{1,0:T(8,128)(2,1)}, bf16[256,384]{1,0:T(8,128)(2,1)}, u32[]{:S(2)}, u32[]{:S(2)}) collective-permute-start(bf16[256,384]{1,0:T(8,128)(2,1)} %copy.326), channel_id=1, source_target_pairs={{0,32},{32,0},{8,40},{40,8},{16,48},{48,16},{24,56},{56,24},{64,96... | collective-permute-start | bytes 589832 | tf_op jit(solution)/shard_map/ppermute | solution.py:17
  559.9 26.9 %collective-permute-start.8 = (bf16[256,384]{1,0:T(8,128)(2,1)S(1)}, bf16[256,384]{1,0:T(8,128)(2,1)S(1)}, u32[]{:S(2)}, u32[]{:S(2)}) collective-permute-start(bf16[256,384]{1,0:T(8,128)(2,1)S(1)} %copy.332), channel_id=1, source_target_pairs={{0,64},{64,0},{8,72},{72,8},{16,80},{80,16},{24,88},{88,24},{32,96... | collective-permute-start | bytes 589832 | tf_op jit(solution)/shard_map/ppermute | solution.py:17
  564.4 24.2 %collective-permute-start.9 = (bf16[256,384]{1,0:T(8,128)(2,1)}, bf16[256,384]{1,0:T(8,128)(2,1)S(1)}, u32[]{:S(2)}, u32[]{:S(2)}) collective-permute-start(bf16[256,384]{1,0:T(8,128)(2,1)} %copy.338), channel_id=1, source_target_pairs={{0,128},{128,0},{8,136},{136,8},{16,144},{144,16},{24,152},{152,24... | collective-permute-start | bytes 589832 | tf_op jit(solution)/shard_map/ppermute | solution.py:17
  579.4 17.0 %copy-start.53 = (bf16[256,384]{1,0:T(8,128)(2,1)S(1)}, bf16[256,384]{1,0:T(8,128)(2,1)}, u32[]{:S(2)}) copy-start(bf16[256,384]{1,0:T(8,128)(2,1)} %param.17) | copy-start | bytes 589828
  579.4 17.0 %copy-start.54 = (bf16[256,256]{1,0:T(8,128)(2,1)S(1)}, bf16[256,256]{1,0:T(8,128)(2,1)}, u32[]{:S(2)}) copy-start(bf16[256,256]{1,0:T(8,128)(2,1)} %get-tuple-element.32) | copy-start | bytes 393220
  581.1 137.9 %copy-start.1 = (bf16[256,768]{1,0:T(8,128)(2,1)S(1)}, bf16[256,768]{1,0:T(8,128)(2,1)}, u32[]{:S(2)}) copy-start(bf16[256,768]{1,0:T(8,128)(2,1)} %param.15) | copy-start | bytes 1179652
  581.9 9.7 %collective-permute-start = (bf16[256,384]{1,0:T(8,128)(2,1)}, bf16[256,384]{1,0:T(8,128)(2,1)S(1)}, u32[]{:S(2)}, u32[]{:S(2)}) collective-permute-start(bf16[256,384]{1,0:T(8,128)(2,1)} %copy.251), channel_id=1, source_target_pairs={{0,8},{8,0},{16,24},{24,16},{32,40},{40,32},{48,56},{56,48},{64,72... | collective-permute-start | bytes 589832 | tf_op jit(solution)/shard_map/ppermute | solution.py:17
  582.5 13.2 %collective-permute-start.1 = (bf16[256,384]{1,0:T(8,128)(2,1)}, bf16[256,384]{1,0:T(8,128)(2,1)S(1)}, u32[]{:S(2)}, u32[]{:S(2)}) collective-permute-start(bf16[256,384]{1,0:T(8,128)(2,1)} %copy.258), channel_id=1, source_target_pairs={{0,16},{16,0},{8,24},{24,8},{32,48},{48,32},{40,56},{56,40},{64,80... | collective-permute-start | bytes 589832 | tf_op jit(solution)/shard_map/ppermute | solution.py:17
  583.8 12.6 %collective-permute-start.2 = (bf16[256,384]{1,0:T(8,128)(2,1)}, bf16[256,384]{1,0:T(8,128)(2,1)S(1)}, u32[]{:S(2)}, u32[]{:S(2)}) collective-permute-start(bf16[256,384]{1,0:T(8,128)(2,1)} %copy.264), channel_id=1, source_target_pairs={{0,32},{32,0},{8,40},{40,8},{16,48},{48,16},{24,56},{56,24},{64,96... | collective-permute-start | bytes 589832 | tf_op jit(solution)/shard_map/ppermute | solution.py:17
  586.8 9.6 %collective-permute-start.3 = (bf16[256,384]{1,0:T(8,128)(2,1)}, bf16[256,384]{1,0:T(8,128)(2,1)S(1)}, u32[]{:S(2)}, u32[]{:S(2)}) collective-permute-start(bf16[256,384]{1,0:T(8,128)(2,1)} %copy.270), channel_id=1, source_target_pairs={{0,64},{64,0},{8,72},{72,8},{16,80},{80,16},{24,88},{88,24},{32,96... | collective-permute-start | bytes 589832 | tf_op jit(solution)/shard_map/ppermute | solution.py:17
  588.6 7.8 %collective-permute-start.4 = (bf16[256,384]{1,0:T(8,128)(2,1)}, bf16[256,384]{1,0:T(8,128)(2,1)S(1)}, u32[]{:S(2)}, u32[]{:S(2)}) collective-permute-start(bf16[256,384]{1,0:T(8,128)(2,1)} %copy.276), channel_id=1, source_target_pairs={{0,128},{128,0},{8,136},{136,8},{16,144},{144,16},{24,152},{152,24... | collective-permute-start | bytes 589832 | tf_op jit(solution)/shard_map/ppermute | solution.py:17
  (47 other events, 246.1 us)
Sparse Core Ops, SparseCore 0:
  12.1 184.8 all-reduce.6
  200.2 85.5 all-gather.1
  359.2 141.2 all-reduce.4
  502.8 36.3 reduce-scatter.8
  542.2 32.1 reduce-scatter.18
  577.4 32.0 reduce-scatter.16
  612.6 32.1 reduce-scatter.12
  648.0 32.1 reduce-scatter.14
  683.4 35.5 reduce-scatter.10
